TPU v7x, 512 devices: a whole 4x8x8 slice. The times are simulated.
512 devices in a mesh: dp: 128 (over y, z, core), grp: 4 (over x).
Axes of the slice: x: 4, y: 8, z: 8, core: 2. Of those that a mesh axis runs over, the one named last changes fastest.
Arguments:
- states: bfloat16 [65536, 2048], P(('dp', 'grp')), may hold values from -60 to 60
- projection: bfloat16 [2048, 768], replicated, may hold values from -0.125 to 0.125
- owner_group: int32 [65536, 1], P(('dp', 'grp')), may hold values from 0 to 127; in each aligned block of 128 rows (0 to 127, 128 to 255, ...) at most 2 rows name the same one
- cluster_sub: int32 [65536], P(('dp', 'grp')), may hold values from 0 to 3
- priority: int32 [65536], P(('dp', 'grp')), may hold values from 0 to 65535, each once
Outputs:
- dup_score: float32 [65536], P(('dp', 'grp'))
Inputs may be any that keep to these rules, and one draw needn't show every extreme that they name: `owner_group`: in each aligned block of 128 rows (the rows of one device) no owner is named by more than 2 rows; in some block some owner is named by exactly 2 rows.
All inputs are finite; a program needn't handle non-finite values.
Results may differ from a plain program's by a relative error of at most 0.0012.
Values may be sent and summed in bfloat16 or wider, within the bound.
A program may use at most 64 MiB of HBM per device.

v0:
```python
import jax
import jax.numpy as jnp
from jax import lax
from jax.sharding import PartitionSpec as P


def pair_tile(query_emb, key_emb):
    return lax.dot_general(
        query_emb, key_emb, (((1,), (1,)), ((), ())), preferred_element_type=jnp.float32
    )


def on_device(states, projection, owner_group, cluster_sub, priority):
    num_dp = lax.axis_size("dp")
    doc_rows = states.shape[0]
    emb_width = projection.shape[1]
    slot_count = max(2, (2 * doc_rows + num_dp - 1) // num_dp)
    recv_rows = num_dp * slot_count
    projected = jnp.dot(states, projection, preferred_element_type=jnp.float32)
    square_sum = jnp.sum(projected * projected, axis=1, keepdims=True)
    inverse_norm = lax.rsqrt(square_sum + 1e-06)
    embedding = (projected * inverse_norm).astype(jnp.bfloat16)
    owner_row = owner_group[:, 0]
    onehot = (owner_row[:, None] == jnp.arange(num_dp, dtype=jnp.int32)[None, :]).astype(jnp.int32)
    slot_place = jnp.sum(onehot * (jnp.cumsum(onehot, axis=0) - 1), axis=1)
    target = owner_row * slot_count + slot_place
    send_emb = jnp.zeros((recv_rows, emb_width), jnp.bfloat16).at[target].set(embedding)
    send_sub = jnp.full((recv_rows,), -1, jnp.int32).at[target].set(cluster_sub)
    send_prio = jnp.zeros((recv_rows,), jnp.int32).at[target].set(priority)
    got_emb, got_sub, got_prio = (
        lax.all_to_all(
            send_emb.reshape(num_dp, slot_count, emb_width),
            "dp",
            split_axis=0,
            concat_axis=0,
            tiled=True,
        ),
        lax.all_to_all(
            send_sub.reshape(num_dp, slot_count), "dp", split_axis=0, concat_axis=0, tiled=True
        ),
        lax.all_to_all(
            send_prio.reshape(num_dp, slot_count), "dp", split_axis=0, concat_axis=0, tiled=True
        ),
    )
    member_emb = got_emb.reshape(recv_rows, emb_width)
    member_sub = got_sub.reshape(recv_rows)
    member_prio = got_prio.reshape(recv_rows)
    lowest = jnp.full((recv_rows,), -1.0, jnp.float32)
    cosine = pair_tile(member_emb, lax.all_gather(member_emb, "grp", axis=0, tiled=True))
    earlier = (
        member_sub[:, None] == lax.all_gather(member_sub, "grp", axis=0, tiled=True)[None, :]
    ) & (lax.all_gather(member_prio, "grp", axis=0, tiled=True)[None, :] < member_prio[:, None])
    running = jnp.maximum(lowest, jnp.max(jnp.where(earlier, cosine, -1.0), axis=1))
    result_back = lax.all_to_all(
        running.reshape(num_dp, slot_count), "dp", split_axis=0, concat_axis=0, tiled=True
    )
    return result_back.reshape(recv_rows)[target]


def solution(mesh):
    in_specs = (
        P(("dp", "grp"), None),
        P(),
        P(("dp", "grp"), None),
        P(("dp", "grp")),
        P(("dp", "grp")),
    )
    out_specs = P(("dp", "grp"))
    return jax.shard_map(
        on_device, mesh=mesh, in_specs=in_specs, out_specs=out_specs, check_vma=False
    )
```

profile of v0, /device:TPU:1, one launch (start us, length us, event | category | flops | bytes accessed | tf_op | source)
XLA Modules:
  0.0 138.6 jit_solution(18221700818211266229)
XLA Ops:
  6.5 0.9 fusion.4
  7.6 0.8 select_reduce_fusion
  9.1 1.7 %multiply_reduce_fusion = (f32[128]{0:T(128)S(1)}, f32[128,768]{1,0:T(8,128)S(1)}) fusion(bf16[128,2048]{1,0:T(8,128)(2,1)} %param.5, bf16[2048,768]{1,0:T(8,128)(2,1)S(1)} %copy-done), kind=kOutput, calls=%fused_computation.7 | convolution fusion | flops 402849664 | bytes 4063744 | tf_op jit(solution)/shard_map/dot_general | solution.py:19
  10.8 1.9 %scatter_custom_fusion.2 = bf16[256,768]{1,0:T(8,128)(2,1)} fusion(s32[128]{0:T(128)S(1)} %fusion.5, f32[128,768]{1,0:T(8,128)S(1)} %get-tuple-element.6, f32[128]{0:T(128)S(1)} %add_rsqrt_fusion, bf16[]{:T(256)} %constant.13.clone.1), kind=kCustom, calls=%fused_computation.8 | custom fusion | flops 196608 | bytes 786946 | tf_op jit(solution)/shard_map/scatter | solution.py:27
  12.7 1.1 reshape.54
  13.9 35.1 %all_to_all.29 = bf16[128,2,768]{2,1,0:T(2,128)(2,1)} all-to-all(bf16[128,2,768]{2,1,0:T(2,128)(2,1)S(1)} %reshape.54), channel_id=1, replica_groups=mesh['dp'=128,'grp'=4] {'dp'}, dimensions={0} | all-to-all | bytes 786432 | tf_op jit(solution)/shard_map/all_to_all | solution.py:31
  49.0 1.9 %reshape.55 = bf16[256,768]{1,0:T(8,128)(2,1)} reshape(bf16[128,2,768]{2,1,0:T(2,128)(2,1)} %all_to_all.29) | data formatting | bytes 786432 | tf_op jit(solution)/shard_map/reshape | solution.py:45
  50.9 1.1 scatter_custom_fusion
  52.0 0.8 all_to_all.19
  52.8 7.1 %all-to-all-start = ((s32[128,1,2]{2,1,0:T(1,128)}), s32[128,1,2]{2,1,0:T(1,128)S(1)}, u32[]{:S(2)}, u32[]{:S(2)}) async-start(s32[128,1,2]{2,1,0:T(1,128)} %bitcast.3), calls=%async_computation | async-start | bytes 131072 | tf_op jit(solution)/shard_map/all_to_all | solution.py:38
  59.9 1.1 scatter_custom_fusion.1
  61.8 9.8 %all-to-all-done = s32[128,1,2]{2,1,0:T(1,128)S(1)} async-done(((s32[128,1,2]{2,1,0:T(1,128)}), s32[128,1,2]{2,1,0:T(1,128)S(1)}, u32[]{:S(2)}, u32[]{:S(2)}) %all-to-all-start) | async-done | bytes 1056 | tf_op jit(solution)/shard_map/all_to_all | solution.py:38
  71.6 5.7 %all-to-all-start.1 = ((s32[128,1,2]{2,1,0:T(1,128)}), s32[128,1,2]{2,1,0:T(1,128)S(1)}, u32[]{:S(2)}, u32[]{:S(2)}) async-start(s32[128,1,2]{2,1,0:T(1,128)} %bitcast.5), calls=%async_computation.1 | async-start | bytes 131072 | tf_op jit(solution)/shard_map/all_to_all | solution.py:41
  77.4 11.5 %all-to-all-done.1 = s32[128,1,2]{2,1,0:T(1,128)S(1)} async-done(((s32[128,1,2]{2,1,0:T(1,128)}), s32[128,1,2]{2,1,0:T(1,128)S(1)}, u32[]{:S(2)}, u32[]{:S(2)}) %all-to-all-start.1) | async-done | bytes 1056 | tf_op jit(solution)/shard_map/all_to_all | solution.py:41
  89.5 0.8 reduce.13
  90.5 0.8 reduce.14
  91.4 7.7 %all-gather = s32[4,1,256]{2,1,0:T(1,128)S(1)} all-gather(s32[1,1,256]{2,1,0:T(1,128)S(1)} %reshape.89), channel_id=1, replica_groups=mesh['dp'=128,'grp'=4] {'grp'}, dimensions={0}, use_global_device_ids=true | all-gather | bytes 5120 | tf_op jit(solution)/shard_map/all_gather | solution.py:51
  99.1 5.2 %all-gather.1 = s32[4,1,256]{2,1,0:T(1,128)S(1)} all-gather(s32[1,1,256]{2,1,0:T(1,128)S(1)} %reshape.91), channel_id=1, replica_groups=mesh['dp'=128,'grp'=4] {'grp'}, dimensions={0}, use_global_device_ids=true | all-gather | bytes 5120 | tf_op jit(solution)/shard_map/all_gather | solution.py:52
  104.3 2.3 %fusion = f32[256]{0:T(256)S(1)} fusion(bf16[256,768]{1,0:T(8,128)(2,1)} %reshape.55, bf16[1024,768]{1,0:T(8,128)(2,1)} %all-gather.4.cloned.1.call-done, s32[1024]{0:T(1024)S(1)} %bitcast.24, s32[1024]{0:T(1024)S(1)} %bitcast.23, s32[256]{0:T(256)S(1)} %reshape.53, s32[256]{0:T(256)S(1)} %eq.34), kind=kOutput, calls=%fused_computation.5 | convolution fusion | flops 403963648 | bytes 1977344 | tf_op jit(solution)/shard_map/dot_general | solution.py:8
  106.6 0.8 max_broadcast_in_dim.15
  107.4 9.5 %all-to-all-start.3 = ((f32[128,1,2]{2,1,0:T(1,128)}), f32[128,1,2]{2,1,0:T(1,128)S(1)}, u32[]{:S(2)}, u32[]{:S(2)}) async-start(f32[128,1,2]{2,1,0:T(1,128)} %bitcast.7), calls=%async_computation.3 | async-start | bytes 131072 | tf_op jit(solution)/shard_map/all_to_all | solution.py:54
  116.9 11.6 %all-to-all-done.3 = f32[128,1,2]{2,1,0:T(1,128)S(1)} async-done(((f32[128,1,2]{2,1,0:T(1,128)}), f32[128,1,2]{2,1,0:T(1,128)S(1)}, u32[]{:S(2)}, u32[]{:S(2)}) %all-to-all-start.3) | async-done | bytes 1056 | tf_op jit(solution)/shard_map/all_to_all | solution.py:54
  129.0 0.8 reduce.15
  130.0 1.8 %gather_fusion = f32[128]{0:T(128)} fusion(f32[256]{0:T(256)S(1)} %reshape.56, s32[1024]{0:T(1024)S(1)} %pad_clamp_fusion), kind=kCustom, calls=%fused_computation | custom fusion | bytes 1536 | tf_op jit(solution)/shard_map/gather | solution.py:57
  (18 shorter events, 3.3 us)
Async XLA Ops:
  6.5 2.6 %copy-start = (bf16[2048,768]{1,0:T(8,128)(2,1)S(1)}, bf16[2048,768]{1,0:T(8,128)(2,1)}, u32[]{:S(2)}) copy-start(bf16[2048,768]{1,0:T(8,128)(2,1)} %param.6) | copy-start | bytes 9437188
  6.5 97.8 %all-gather.4.cloned.1.call-start = ((), (), s32[]{:S(2)}) async-start(), calls=%async_computation.4 | async-start | bytes 1966080 | tf_op jit(solution)/shard_map/all_gather | solution.py:49
  52.8 18.8 %all-to-all-start = ((s32[128,1,2]{2,1,0:T(1,128)}), s32[128,1,2]{2,1,0:T(1,128)S(1)}, u32[]{:S(2)}, u32[]{:S(2)}) async-start(s32[128,1,2]{2,1,0:T(1,128)} %bitcast.3), calls=%async_computation | async-start | bytes 131072 | tf_op jit(solution)/shard_map/all_to_all | solution.py:38
  71.6 17.3 %all-to-all-start.1 = ((s32[128,1,2]{2,1,0:T(1,128)}), s32[128,1,2]{2,1,0:T(1,128)S(1)}, u32[]{:S(2)}, u32[]{:S(2)}) async-start(s32[128,1,2]{2,1,0:T(1,128)} %bitcast.5), calls=%async_computation.1 | async-start | bytes 131072 | tf_op jit(solution)/shard_map/all_to_all | solution.py:41
  107.4 21.1 %all-to-all-start.3 = ((f32[128,1,2]{2,1,0:T(1,128)}), f32[128,1,2]{2,1,0:T(1,128)S(1)}, u32[]{:S(2)}, u32[]{:S(2)}) async-start(f32[128,1,2]{2,1,0:T(1,128)} %bitcast.7), calls=%async_computation.3 | async-start | bytes 131072 | tf_op jit(solution)/shard_map/all_to_all | solution.py:54
Sparse Core Ops, SparseCore 0:
  51.0 25.2 all-gather.3
where the time goes:
time: 139 us
  blocking collectives  48.1 us (35%)
  waiting for transfers between devices  32.9 us (24%)
  starting transfers between devices  22.3 us (16%)
  between operations  13.5 us (10%)
  local copies, waits for them, and re-layouts  11 us (8%)
  other arithmetic  6.92 us (5%)
  matrix products  3.96 us (3%)
    all_to_all x1, blocking collectives, on_device(): lax.all_to_all(send_emb.reshape(num_dp, slot_count, emb_width), 'dp', spl...  35.1 us
    all_to_all x1, waiting for transfers between devices, on_device(): lax.all_to_all(running.reshape(num_dp, slot_count), 'dp', split_axis=0, c...  11.6 us
    all_to_all x1, waiting for transfers between devices, on_device(): lax.all_to_all(send_prio.reshape(num_dp, slot_count), 'dp', split_axis=0,...  11.5 us
    all_to_all x1, waiting for transfers between devices, on_device(): lax.all_to_all(send_sub.reshape(num_dp, slot_count), 'dp', split_axis=0,...  9.76 us
    all_to_all x1, starting transfers between devices, on_device(): lax.all_to_all(running.reshape(num_dp, slot_count), 'dp', split_axis=0, c...  9.48 us
    all_gather x1, blocking collectives, on_device(): lax.all_gather(member_sub, 'grp', axis=0, tiled=True)[None, :]  7.71 us
    all_to_all x1, starting transfers between devices, on_device(): lax.all_to_all(send_sub.reshape(num_dp, slot_count), 'dp', split_axis=0,...  7.12 us
    all_to_all x1, starting transfers between devices, on_device(): lax.all_to_all(send_prio.reshape(num_dp, slot_count), 'dp', split_axis=0,...  5.65 us
  transfers between devices with their start and end apart: 4, of which 3 were waited for; matrix products, arithmetic and copies ran while one was open for 4% of the time, Pallas kernels for 0%

commit v1 on v0

--- a/solution.py
+++ b/solution.py
@@ -2,6 +2,11 @@
 import jax.numpy as jnp
 from jax import lax
 from jax.sharding import PartitionSpec as P
+
+
+def tiled_gather(shard, axis, dim):
+    copies = jnp.concatenate([shard] * lax.axis_size(axis), axis=dim)
+    return lax.all_to_all(copies, axis, dim, dim, tiled=True)
 
 
 def pair_tile(query_emb, key_emb):
@@ -47,9 +52,9 @@
     member_prio = got_prio.reshape(recv_rows)
     lowest = jnp.full((recv_rows,), -1.0, jnp.float32)
     cosine = pair_tile(member_emb, lax.all_gather(member_emb, "grp", axis=0, tiled=True))
-    earlier = (
-        member_sub[:, None] == lax.all_gather(member_sub, "grp", axis=0, tiled=True)[None, :]
-    ) & (lax.all_gather(member_prio, "grp", axis=0, tiled=True)[None, :] < member_prio[:, None])
+    earlier = (member_sub[:, None] == tiled_gather(member_sub, "grp", 0)[None, :]) & (
+        lax.all_gather(member_prio, "grp", axis=0, tiled=True)[None, :] < member_prio[:, None]
+    )
     running = jnp.maximum(lowest, jnp.max(jnp.where(earlier, cosine, -1.0), axis=1))
     result_back = lax.all_to_all(
         running.reshape(num_dp, slot_count), "dp", split_axis=0, concat_axis=0, tiled=True

time: 139 us -> 136 us (0.978)
  blocking collectives: 48.1 us -> 43 us
  starting transfers between devices: 22.3 us -> 25.1 us
    all_gather x1 -> x0, blocking collectives: 7.71 us -> none  [on_device(): lax.all_gather(member_sub, 'grp', axis=0, tiled=True)[None, :]]
    all_to_all x0 -> x1, starting transfers between devices: none -> 4.02 us  [tiled_gather(): return lax.all_to_all(copies, axis, dim, dim, tiled=True)]
    all_gather x1, blocking collectives: 5.23 us -> 7.9 us  [on_device(): lax.all_gather(member_prio, 'grp', axis=0, tiled=True)[None, :]]
  transfers between devices with their start and end apart: 4 -> 5, of which waited for: 3 -> 3; matrix products, arithmetic and copies ran while one was open for 4% -> 4% of each run, Pallas kernels for 0% -> 0%
where the time goes in v1:
time: 136 us
  blocking collectives  43 us (32%)
  waiting for transfers between devices  31.6 us (23%)
  starting transfers between devices  25.1 us (18%)
  between operations  13.5 us (10%)
  local copies, waits for them, and re-layouts  11.5 us (8%)
  other arithmetic  6.92 us (5%)
  matrix products  3.96 us (3%)
    all_to_all x1, blocking collectives, on_device(): lax.all_to_all(send_emb.reshape(num_dp, slot_count, emb_width), 'dp', spl...  35.1 us
    all_to_all x1, waiting for transfers between devices, on_device(): lax.all_to_all(running.reshape(num_dp, slot_count), 'dp', split_axis=0, c...  11.6 us
    all_to_all x1, waiting for transfers between devices, on_device(): lax.all_to_all(send_prio.reshape(num_dp, slot_count), 'dp', split_axis=0,...  10.2 us
    all_to_all x1, waiting for transfers between devices, on_device(): lax.all_to_all(send_sub.reshape(num_dp, slot_count), 'dp', split_axis=0,...  9.76 us
    all_to_all x1, starting transfers between devices, on_device(): lax.all_to_all(running.reshape(num_dp, slot_count), 'dp', split_axis=0, c...  8.31 us
    all_gather x1, blocking collectives, on_device(): lax.all_gather(member_prio, 'grp', axis=0, tiled=True)[None, :]  7.9 us
    all_to_all x1, starting transfers between devices, on_device(): lax.all_to_all(send_sub.reshape(num_dp, slot_count), 'dp', split_axis=0,...  7.12 us
    all_to_all x1, starting transfers between devices, on_device(): lax.all_to_all(send_prio.reshape(num_dp, slot_count), 'dp', split_axis=0,...  5.65 us
  transfers between devices with their start and end apart: 5, of which 3 were waited for; matrix products, arithmetic and copies ran while one was open for 4% of the time, Pallas kernels for 0%

profile of v1, /device:TPU:1, one launch (start us, length us, event | category | flops | bytes accessed | tf_op | source)
XLA Modules:
  0.0 135.5 jit_solution(10363941797466229855)
XLA Ops:
  6.5 0.9 fusion.4
  7.6 0.8 select_reduce_fusion
  9.1 1.7 %multiply_reduce_fusion = (f32[128]{0:T(128)S(1)}, f32[128,768]{1,0:T(8,128)S(1)}) fusion(bf16[128,2048]{1,0:T(8,128)(2,1)} %param.5, bf16[2048,768]{1,0:T(8,128)(2,1)S(1)} %copy-done), kind=kOutput, calls=%fused_computation.7 | convolution fusion | flops 402849664 | bytes 4063744 | tf_op jit(solution)/shard_map/dot_general | solution.py:24
  10.8 1.9 %scatter_custom_fusion.2 = bf16[256,768]{1,0:T(8,128)(2,1)} fusion(s32[128]{0:T(128)S(1)} %fusion.5, f32[128,768]{1,0:T(8,128)S(1)} %get-tuple-element.6, f32[128]{0:T(128)S(1)} %add_rsqrt_fusion, bf16[]{:T(256)} %constant.13.clone.1), kind=kCustom, calls=%fused_computation.8 | custom fusion | flops 196608 | bytes 786946 | tf_op jit(solution)/shard_map/scatter | solution.py:32
  12.7 1.1 reshape.69
  13.9 35.1 %all_to_all.35 = bf16[128,2,768]{2,1,0:T(2,128)(2,1)} all-to-all(bf16[128,2,768]{2,1,0:T(2,128)(2,1)S(1)} %reshape.69), channel_id=1, replica_groups=mesh['dp'=128,'grp'=4] {'dp'}, dimensions={0} | all-to-all | bytes 786432 | tf_op jit(solution)/shard_map/all_to_all | solution.py:36
  49.0 1.9 %reshape.70 = bf16[256,768]{1,0:T(8,128)(2,1)} reshape(bf16[128,2,768]{2,1,0:T(2,128)(2,1)} %all_to_all.35) | data formatting | bytes 786432 | tf_op jit(solution)/shard_map/reshape | solution.py:50
  50.9 1.1 scatter_custom_fusion
  52.0 0.8 all_to_all.23
  52.8 7.1 %all-to-all-start = ((s32[128,1,2]{2,1,0:T(1,128)}), s32[128,1,2]{2,1,0:T(1,128)S(1)}, u32[]{:S(2)}, u32[]{:S(2)}) async-start(s32[128,1,2]{2,1,0:T(1,128)} %bitcast.3), calls=%async_computation | async-start | bytes 131072 | tf_op jit(solution)/shard_map/all_to_all | solution.py:43
  59.9 1.1 scatter_custom_fusion.1
  61.8 9.8 %all-to-all-done = s32[128,1,2]{2,1,0:T(1,128)S(1)} async-done(((s32[128,1,2]{2,1,0:T(1,128)}), s32[128,1,2]{2,1,0:T(1,128)S(1)}, u32[]{:S(2)}, u32[]{:S(2)}) %all-to-all-start) | async-done | bytes 1056 | tf_op jit(solution)/shard_map/all_to_all | solution.py:43
  71.6 5.7 %all-to-all-start.2 = ((s32[128,1,2]{2,1,0:T(1,128)}), s32[128,1,2]{2,1,0:T(1,128)S(1)}, u32[]{:S(2)}, u32[]{:S(2)}) async-start(s32[128,1,2]{2,1,0:T(1,128)} %bitcast.5), calls=%async_computation.2 | async-start | bytes 131072 | tf_op jit(solution)/shard_map/all_to_all | solution.py:46
  77.7 0.8 reduce.12
  78.7 10.2 %all-to-all-done.2 = s32[128,1,2]{2,1,0:T(1,128)S(1)} async-done(((s32[128,1,2]{2,1,0:T(1,128)}), s32[128,1,2]{2,1,0:T(1,128)S(1)}, u32[]{:S(2)}, u32[]{:S(2)}) %all-to-all-start.2) | async-done | bytes 1056 | tf_op jit(solution)/shard_map/all_to_all | solution.py:46
  89.4 4.0 %all-to-all-start.1 = ((s32[4,256,1]{1,2,0:T(1,128)}), s32[4,256,1]{1,2,0:T(1,128)S(1)}, u32[]{:S(2)}, u32[]{:S(2)}) async-start(s32[4,256,1]{1,2,0:T(1,128)} %concatenate.4), calls=%async_computation.1 | async-start | bytes 8192 | tf_op jit(solution)/shard_map/all_to_all | solution.py:9
  93.6 0.8 reduce.11
  94.6 7.9 %all-gather = s32[4,1,256]{2,1,0:T(1,128)S(1)} all-gather(s32[1,1,256]{2,1,0:T(1,128)S(1)} %reshape.104), channel_id=1, replica_groups=mesh['dp'=128,'grp'=4] {'grp'}, dimensions={0}, use_global_device_ids=true | all-gather | bytes 5120 | tf_op jit(solution)/shard_map/all_gather | solution.py:56
  102.5 2.3 %fusion = f32[256]{0:T(256)S(1)} fusion(bf16[256,768]{1,0:T(8,128)(2,1)} %reshape.70, bf16[1024,768]{1,0:T(8,128)(2,1)} %all-gather.3.cloned.1.call-done, s32[1024]{0:T(1024)S(1)} %bitcast.21, s32[1024]{0:T(1024)S(1)} %bitcast.22, s32[256]{0:T(256)S(1)} %reshape.68, s32[256]{0:T(256)S(1)} %eq.36), kind=kOutput, calls=%fused_computation.5 | convolution fusion | flops 403963648 | bytes 1977344 | tf_op jit(solution)/shard_map/dot_general | solution.py:13
  104.7 0.8 max_broadcast_in_dim.15
  105.5 8.3 %all-to-all-start.4 = ((f32[128,1,2]{2,1,0:T(1,128)}), f32[128,1,2]{2,1,0:T(1,128)S(1)}, u32[]{:S(2)}, u32[]{:S(2)}) async-start(f32[128,1,2]{2,1,0:T(1,128)} %bitcast.7), calls=%async_computation.4 | async-start | bytes 131072 | tf_op jit(solution)/shard_map/all_to_all | solution.py:59
  113.8 11.6 %all-to-all-done.4 = f32[128,1,2]{2,1,0:T(1,128)S(1)} async-done(((f32[128,1,2]{2,1,0:T(1,128)}), f32[128,1,2]{2,1,0:T(1,128)S(1)}, u32[]{:S(2)}, u32[]{:S(2)}) %all-to-all-start.4) | async-done | bytes 1056 | tf_op jit(solution)/shard_map/all_to_all | solution.py:59
  126.0 0.8 reduce.13
  126.9 1.8 %gather_fusion = f32[128]{0:T(128)} fusion(f32[256]{0:T(256)S(1)} %reshape.71, s32[1024]{0:T(1024)S(1)} %pad_clamp_fusion), kind=kCustom, calls=%fused_computation | custom fusion | bytes 1536 | tf_op jit(solution)/shard_map/gather | solution.py:62
  (19 shorter events, 3.8 us)
Async XLA Ops:
  6.5 2.6 %copy-start = (bf16[2048,768]{1,0:T(8,128)(2,1)S(1)}, bf16[2048,768]{1,0:T(8,128)(2,1)}, u32[]{:S(2)}) copy-start(bf16[2048,768]{1,0:T(8,128)(2,1)} %param.6) | copy-start | bytes 9437188
  6.5 95.9 %all-gather.3.cloned.1.call-start = ((), (), s32[]{:S(2)}) async-start(), calls=%async_computation.5 | async-start | bytes 1966080 | tf_op jit(solution)/shard_map/all_gather | solution.py:54
  52.8 18.8 %all-to-all-start = ((s32[128,1,2]{2,1,0:T(1,128)}), s32[128,1,2]{2,1,0:T(1,128)S(1)}, u32[]{:S(2)}, u32[]{:S(2)}) async-start(s32[128,1,2]{2,1,0:T(1,128)} %bitcast.3), calls=%async_computation | async-start | bytes 131072 | tf_op jit(solution)/shard_map/all_to_all | solution.py:43
  71.6 17.3 %all-to-all-start.2 = ((s32[128,1,2]{2,1,0:T(1,128)}), s32[128,1,2]{2,1,0:T(1,128)S(1)}, u32[]{:S(2)}, u32[]{:S(2)}) async-start(s32[128,1,2]{2,1,0:T(1,128)} %bitcast.5), calls=%async_computation.2 | async-start | bytes 131072 | tf_op jit(solution)/shard_map/all_to_all | solution.py:46
  89.4 13.0 %all-to-all-start.1 = ((s32[4,256,1]{1,2,0:T(1,128)}), s32[4,256,1]{1,2,0:T(1,128)S(1)}, u32[]{:S(2)}, u32[]{:S(2)}) async-start(s32[4,256,1]{1,2,0:T(1,128)} %concatenate.4), calls=%async_computation.1 | async-start | bytes 8192 | tf_op jit(solution)/shard_map/all_to_all | solution.py:9
  105.5 20.0 %all-to-all-start.4 = ((f32[128,1,2]{2,1,0:T(1,128)}), f32[128,1,2]{2,1,0:T(1,128)S(1)}, u32[]{:S(2)}, u32[]{:S(2)}) async-start(f32[128,1,2]{2,1,0:T(1,128)} %bitcast.7), calls=%async_computation.4 | async-start | bytes 131072 | tf_op jit(solution)/shard_map/all_to_all | solution.py:59
Sparse Core Ops, SparseCore 0:
  51.0 25.2 all-gather.2
